TPU v7x, 32 devices: a whole 2x2x4 slice. The times are simulated.
32 devices in a mesh: dp: 2 (over y), section: 4 (over z), mp: 4 (over x, core).
Axes of the slice: x: 2, y: 2, z: 4, core: 2. Of those that a mesh axis runs over, the one named last changes fastest.
Arguments:
- token_ids: int32 [32, 32], P('dp'), may hold values from 0 to 65535
- members: int32 [32], replicated, may hold values from 0 to 31, each once
- owners: int32 [4], replicated, may hold values from 0 to 3, each once
- embed_table: bfloat16 [4096, 65536], P('mp', 'section'), may hold values from -6 to 6
- norm_gain: float32 [4, 4096], P('section'), may hold values from 0.5 to 2
- gate_weight: bfloat16 [4, 4096, 10240], P('section', None, 'mp'), may hold values from -0.09375 to 0.09375
- up_weight: bfloat16 [4, 4096, 10240], P('section', None, 'mp'), may hold values from -0.09375 to 0.09375
- down_weight: bfloat16 [4, 4096, 10240], P('section', None, 'mp'), may hold values from -0.078125 to 0.078125
- final_gain: float32 [4096], replicated, may hold values from 0.5 to 2
- head_weight: bfloat16 [4096, 4096], P(None, 'mp'), may hold values from -0.0014648438 to 0.0014648438
Outputs:
- wins: float32 [4, 8, 8], P('dp', 'section')
Inputs may be any that keep to these rules, and one draw needn't show every extreme that they name: Prompt p's responses are members[8 * p] to members[8 * p + 7]; each response belongs to one prompt. `owners`: each slot holds one prompt.
All inputs are finite; a program needn't handle non-finite values.
Results may differ from a plain program's by a relative error of at most 0.028.
Values may be sent and summed in bfloat16 or wider, within the bound.
A program may use at most 192 MiB of HBM per device.

v0:
```python
import jax
import jax.numpy as jnp
from jax import lax
from jax.sharding import PartitionSpec as P

GROUP = 8
norm_eps = 1e-05
final_eps = 1e-06


def passed_along(value, axis, steps):
    count = lax.axis_size(axis)
    leading, last = (max(0, -steps), min(count, count - steps))
    return lax.ppermute(value, axis, [(source, source + steps) for source in range(leading, last)])


def broadcast(block, axis, source):
    block = jnp.where(lax.axis_index(axis) == source, block, jnp.zeros_like(block))
    return lax.psum(block, axis)


def contract_rows(weights, acts):
    return lax.dot_general(
        weights, acts, (((0,), (0,)), ((), ())), preferred_element_type=jnp.float32
    )


def activate(gate_acc, up_acc, squares, width):
    inverse = lax.rsqrt(squares / width + norm_eps)
    return (jax.nn.silu(gate_acc * inverse) * (up_acc * inverse)).astype(jnp.bfloat16)


def layer_split(state, gain, w_gate, w_up, w_down):
    width = gain.shape[0]
    wide = lax.all_gather(state, "mp", axis=0, tiled=True).astype(jnp.float32)
    scaled = (wide * gain[:, None]).astype(jnp.bfloat16)
    gate_acc = contract_rows(w_gate, scaled)
    up_acc = contract_rows(w_up, scaled)
    squares = jnp.sum(wide * wide, axis=0, keepdims=True)
    gate_acc, up_acc, squares = (gate_acc, up_acc, squares)
    hidden = activate(gate_acc, up_acc, squares, width)
    mixed = lax.psum_scatter(
        jnp.dot(w_down, hidden, preferred_element_type=jnp.float32).astype(jnp.bfloat16),
        "mp",
        scatter_dimension=0,
        tiled=True,
    ).astype(jnp.float32)
    return (state.astype(jnp.float32) + mixed).astype(jnp.bfloat16)


def per_device(
    token_ids,
    members,
    owners,
    embed_table,
    norm_gain,
    gate_weight,
    up_weight,
    down_weight,
    final_gain,
    head_weight,
):
    sections = lax.axis_size("section")
    section = lax.axis_index("section")
    vocab_part = embed_table.shape[1]
    flat = token_ids.reshape(-1)
    local_ids = flat - section * vocab_part
    inside = (local_ids >= 0) & (local_ids < vocab_part)
    picked = jnp.take(embed_table, jnp.clip(local_ids, 0, vocab_part - 1), axis=1)
    partial_value = jnp.where(inside[None, :], picked.astype(jnp.float32), 0.0)
    embedded = lax.psum(partial_value.astype(jnp.bfloat16), "section")
    gain = norm_gain[0]
    w_gate = gate_weight[0]
    w_up = up_weight[0]
    w_down = down_weight[0]
    block = embedded.shape[1] // sections
    state = jnp.zeros((embedded.shape[0], block), jnp.bfloat16)
    finished = []
    for tick in range(sections + sections - 1):
        if tick < sections:
            fresh = embedded[:, tick * block : (tick + 1) * block]
            state = jnp.where(section == 0, fresh, state)
        result = layer_split(state, gain, w_gate, w_up, w_down)
        if tick >= sections - 1:
            finished.append(result)
        if tick < sections + sections - 2:
            state = passed_along(result, "section", 1)
    final = jnp.concatenate(finished, axis=1)
    responses_here = token_ids.shape[0]
    length = token_ids.shape[1]
    pooled = jnp.mean(
        final.astype(jnp.float32).reshape(final.shape[0], responses_here, length), axis=2
    )
    groups_count = lax.axis_size("dp")
    parts = lax.axis_size("mp")
    stacked = lax.all_gather(pooled[None], ("dp", "mp"), axis=0, tiled=True)
    stacked = stacked.reshape(groups_count, parts, pooled.shape[0], responses_here)
    everyone = jnp.transpose(stacked, (1, 2, 0, 3)).reshape(
        parts * pooled.shape[0], groups_count * responses_here
    )
    factor = lax.rsqrt(jnp.mean(everyone * everyone, axis=0, keepdims=True) + final_eps)
    normed = (everyone * factor * final_gain[:, None]).astype(jnp.bfloat16)
    head_cols = head_weight.shape[1]
    projected = contract_rows(head_weight, normed)
    mine = lax.dynamic_slice_in_dim(normed, lax.axis_index("mp") * head_cols, head_cols).astype(
        jnp.float32
    )
    partial_scores = lax.dot_general(
        projected,
        mine,
        (((0,), (0,)), ((), ())),
        precision=lax.Precision.HIGHEST,
        preferred_element_type=jnp.float32,
    )
    scores = lax.psum(partial_scores, "mp")
    scores = broadcast(scores, "section", sections - 1)
    preference = jax.nn.sigmoid(scores - scores.T)
    prompt_count = owners.shape[0]
    local_prompts = prompt_count // lax.axis_size("dp")
    rows_local = GROUP // sections
    slot_here = lax.axis_index("dp") * local_prompts + jnp.arange(local_prompts, dtype=jnp.int32)
    match = (owners[None, :] == slot_here[:, None]).astype(jnp.int32)
    prompt_here = jnp.sum(match * jnp.arange(prompt_count, dtype=jnp.int32)[None, :], axis=1)
    groups = members.reshape(prompt_count, GROUP)
    chosen = groups[prompt_here]
    row_ids = lax.dynamic_slice_in_dim(chosen, section * rows_local, rows_local, 1)
    return preference[row_ids[:, :, None], chosen[:, None, :]]


def solution(mesh):
    placed = (
        P("dp", None),
        P(),
        P(),
        P("mp", "section"),
        P("section", None),
        P("section", None, "mp"),
        P("section", None, "mp"),
        P("section", None, "mp"),
        P(),
        P(None, "mp"),
    )
    return jax.shard_map(
        per_device, mesh=mesh, in_specs=placed, out_specs=P("dp", "section", None), check_vma=False
    )
```

profile of v0, /device:TPU:0, one launch (start us, length us, event | category | flops | bytes accessed | tf_op | source)
XLA Modules:
  0.0 752.2 jit_solution(12075295378497106360)
XLA Ops:
  8.2 43.9 %copy.26 = bf16[1024,16384]{0,1:T(8,128)(2,1)} copy(bf16[1024,16384]{1,0:T(8,128)(2,1)} %param.13) | data formatting | bytes 67108864 | tf_op args[3]
  52.1 16.3 %gather_fusion = bf16[512,1024]{1,0:T(8,128)(2,1)S(1)} fusion(bf16[1024,16384]{0,1:T(8,128)(2,1)} %copy.26, s32[1024]{0:T(1024)S(1)} %pad_clamp_fusion.1), kind=kCustom, calls=%fused_computation | custom fusion | bytes 2099200 | tf_op jit(solution)/shard_map/jit(_take)/gather | solution.py:69
  69.9 54.7 %all-reduce.2.cloned.1.call-done = bf16[1024,512]{0,1:T(8,128)(2,1)} async-done(((bf16[1024,512]{0,1:T(8,128)(2,1)}), bf16[1024,512]{0,1:T(8,128)(2,1)}) %all-reduce.2.cloned.1.call-update) | async-done | bytes 1048592 | tf_op jit(solution)/shard_map/psum | solution.py:71
  124.6 1.7 slice_select_fusion
  126.3 16.1 %all-gather.9.cloned.1.call-done = bf16[4096,128]{0,1:T(8,128)(2,1)} async-done(((bf16[1024,128]{0,1:T(8,128)(2,1)}), bf16[4096,128]{0,1:T(8,128)(2,1)}) %all-gather.9.cloned.1.call-update) | async-done | bytes 1048592 | tf_op jit(solution)/shard_map/all_gather | solution.py:35
  143.9 11.3 %fusion.87 = f32[2560,128]{0,1:T(8,128)} fusion(bf16[1,4096,2560]{2,1,0:T(8,128)(2,1)} %param.15, bf16[4096,128]{0,1:T(8,128)(2,1)} %all-gather.9.cloned.1.call-done, f32[4096]{0:T(1024)S(1)} %bitcast.292, f32[128]{0:T(128)S(1)} %add_rsqrt_fusion.7), kind=kOutput, calls=%fused_computation.60 | convolution fusion | flops 2686255104 | bytes 23347712 | tf_op jit(solution)/shard_map/dot_general | solution.py:23
  155.3 18.6 %fusion.81 = bf16[4096,128]{0,1:T(8,128)(2,1)} fusion(bf16[1,4096,2560]{2,1,0:T(8,128)(2,1)} %param.17, bf16[1,4096,2560]{2,1,0:T(8,128)(2,1)} %param.16, f32[2560,128]{0,1:T(8,128)} %fusion.87, bf16[4096,128]{0,1:T(8,128)(2,1)S(1)} %copy-done, f32[4096]{0:T(1024)S(1)} %bitcast.293, f32[128]{0:T(128)S(1)} %add_rsqrt_fusion.7), kind=kOutput, calls=%fused_computation.58 | convolution fusion | flops 5373100032 | bytes 45367808 | tf_op jit(solution)/shard_map/dot_general | solution.py:43
  173.9 24.9 %reduce-scatter.8.cloned.1.call-done = bf16[1024,128]{0,1:T(8,128)(2,1)} async-done(((bf16[4096,128]{0,1:T(8,128)(2,1)}), bf16[1024,128]{0,1:T(8,128)(2,1)}) %reduce-scatter.8.cloned.1.call-update) | async-done | bytes 262160 | tf_op jit(solution)/shard_map/reduce_scatter | solution.py:42
  199.9 3.4 collective-permute-start
  203.3 5.4 collective-permute-done
  210.0 17.3 %all-gather.11.cloned.1.call-done = bf16[4096,128]{0,1:T(8,128)(2,1)} async-done(((bf16[1024,128]{0,1:T(8,128)(2,1)}), bf16[4096,128]{0,1:T(8,128)(2,1)}) %all-gather.11.cloned.1.call-update) | async-done | bytes 1048592 | tf_op jit(solution)/shard_map/all_gather | solution.py:35
  228.8 11.3 %fusion.93 = f32[2560,128]{0,1:T(8,128)} fusion(bf16[1,4096,2560]{2,1,0:T(8,128)(2,1)} %param.15, bf16[4096,128]{0,1:T(8,128)(2,1)} %all-gather.11.cloned.1.call-done, f32[4096]{0:T(1024)S(1)} %bitcast.294, f32[128]{0:T(128)S(1)} %add_rsqrt_fusion.6), kind=kOutput, calls=%fused_computation.62 | convolution fusion | flops 2686255104 | bytes 23347712 | tf_op jit(solution)/shard_map/dot_general | solution.py:23
  240.1 18.5 %fusion.78 = bf16[4096,128]{0,1:T(8,128)(2,1)} fusion(bf16[1,4096,2560]{2,1,0:T(8,128)(2,1)} %param.17, bf16[1,4096,2560]{2,1,0:T(8,128)(2,1)} %param.16, f32[2560,128]{0,1:T(8,128)} %fusion.93, bf16[4096,128]{0,1:T(8,128)(2,1)S(1)} %copy-done.1, f32[4096]{0:T(1024)S(1)} %bitcast.295, f32[128]{0:T(128)S(1)} %add_rsqrt_fusion.6), kind=kOutput, calls=%fused_computation.57 | convolution fusion | flops 5373100032 | bytes 45367808 | tf_op jit(solution)/shard_map/dot_general | solution.py:43
  258.7 24.9 %reduce-scatter.10.cloned.1.call-done = bf16[1024,128]{0,1:T(8,128)(2,1)} async-done(((bf16[4096,128]{0,1:T(8,128)(2,1)}), bf16[1024,128]{0,1:T(8,128)(2,1)}) %reduce-scatter.10.cloned.1.call-update) | async-done | bytes 262160 | tf_op jit(solution)/shard_map/reduce_scatter | solution.py:42
  284.6 3.4 collective-permute-start.1
  288.0 5.4 collective-permute-done.1
  294.2 17.8 %all-gather.13.cloned.1.call-done = bf16[4096,128]{0,1:T(8,128)(2,1)} async-done(((bf16[1024,128]{0,1:T(8,128)(2,1)}), bf16[4096,128]{0,1:T(8,128)(2,1)}) %all-gather.13.cloned.1.call-update) | async-done | bytes 1048592 | tf_op jit(solution)/shard_map/all_gather | solution.py:35
  313.6 11.3 %fusion.99 = f32[2560,128]{0,1:T(8,128)} fusion(bf16[1,4096,2560]{2,1,0:T(8,128)(2,1)} %param.15, bf16[4096,128]{0,1:T(8,128)(2,1)} %all-gather.13.cloned.1.call-done, f32[4096]{0:T(1024)S(1)} %bitcast.296, f32[128]{0:T(128)S(1)} %add_rsqrt_fusion.5), kind=kOutput, calls=%fused_computation.64 | convolution fusion | flops 2686255104 | bytes 23347712 | tf_op jit(solution)/shard_map/dot_general | solution.py:23
  324.9 18.5 %fusion.75 = bf16[4096,128]{0,1:T(8,128)(2,1)} fusion(bf16[1,4096,2560]{2,1,0:T(8,128)(2,1)} %param.17, bf16[1,4096,2560]{2,1,0:T(8,128)(2,1)} %param.16, f32[2560,128]{0,1:T(8,128)} %fusion.99, bf16[4096,128]{0,1:T(8,128)(2,1)S(1)} %copy-done.2, f32[4096]{0:T(1024)S(1)} %bitcast.297, f32[128]{0:T(128)S(1)} %add_rsqrt_fusion.5), kind=kOutput, calls=%fused_computation.56 | convolution fusion | flops 5373100032 | bytes 45367808 | tf_op jit(solution)/shard_map/dot_general | solution.py:43
  343.7 24.7 %reduce-scatter.12.cloned.1.call-done = bf16[1024,128]{0,1:T(8,128)(2,1)} async-done(((bf16[4096,128]{0,1:T(8,128)(2,1)}), bf16[1024,128]{0,1:T(8,128)(2,1)}) %reduce-scatter.12.cloned.1.call-update) | async-done | bytes 262160 | tf_op jit(solution)/shard_map/reduce_scatter | solution.py:42
  369.4 3.4 collective-permute-start.2
  372.8 5.3 collective-permute-done.2
  379.0 17.8 %all-gather.15.cloned.1.call-done = bf16[4096,128]{0,1:T(8,128)(2,1)} async-done(((bf16[1024,128]{0,1:T(8,128)(2,1)}), bf16[4096,128]{0,1:T(8,128)(2,1)}) %all-gather.15.cloned.1.call-update) | async-done | bytes 1048592 | tf_op jit(solution)/shard_map/all_gather | solution.py:35
  398.3 8.9 %fusion.105 = f32[2560,128]{0,1:T(8,128)S(1)} fusion(bf16[1,4096,2560]{2,1,0:T(8,128)(2,1)} %param.15, bf16[4096,128]{0,1:T(8,128)(2,1)} %all-gather.15.cloned.1.call-done, f32[4096]{0:T(1024)S(1)} %bitcast.298, f32[128]{0:T(128)S(1)} %add_rsqrt_fusion.4), kind=kOutput, calls=%fused_computation.66 | convolution fusion | flops 2686255104 | bytes 23347712 | tf_op jit(solution)/shard_map/dot_general | solution.py:23
  407.3 18.3 %fusion.72 = bf16[4096,128]{0,1:T(8,128)(2,1)} fusion(bf16[1,4096,2560]{2,1,0:T(8,128)(2,1)} %param.17, bf16[1,4096,2560]{2,1,0:T(8,128)(2,1)} %param.16, f32[2560,128]{0,1:T(8,128)S(1)} %fusion.105, bf16[4096,128]{0,1:T(8,128)(2,1)S(1)} %copy-done.3, f32[4096]{0:T(1024)S(1)} %bitcast.299, f32[128]{0:T(128)S(1)} %add_rsqrt_fusion.4), kind=kOutput, calls=%fused_computation.55 | convolution fusion | flops 5373100032 | bytes 45367808 | tf_op jit(solution)/shard_map/dot_general | solution.py:43
  425.7 24.9 %reduce-scatter.14.cloned.1.call-done = bf16[1024,128]{0,1:T(8,128)(2,1)} async-done(((bf16[4096,128]{0,1:T(8,128)(2,1)}), bf16[1024,128]{0,1:T(8,128)(2,1)}) %reduce-scatter.14.cloned.1.call-update) | async-done | bytes 262160 | tf_op jit(solution)/shard_map/reduce_scatter | solution.py:42
  451.6 3.4 collective-permute-start.3
  455.0 5.4 collective-permute-done.3
  461.1 17.8 %all-gather.17.cloned.1.call-done = bf16[4096,128]{0,1:T(8,128)(2,1)} async-done(((bf16[1024,128]{0,1:T(8,128)(2,1)}), bf16[4096,128]{0,1:T(8,128)(2,1)}) %all-gather.17.cloned.1.call-update) | async-done | bytes 1048592 | tf_op jit(solution)/shard_map/all_gather | solution.py:35
  480.5 8.9 %fusion.111 = f32[2560,128]{0,1:T(8,128)S(1)} fusion(bf16[1,4096,2560]{2,1,0:T(8,128)(2,1)} %param.15, bf16[4096,128]{0,1:T(8,128)(2,1)} %all-gather.17.cloned.1.call-done, f32[4096]{0:T(1024)S(1)} %bitcast.300, f32[128]{0:T(128)S(1)} %add_rsqrt_fusion.3), kind=kOutput, calls=%fused_computation.68 | convolution fusion | flops 2686255104 | bytes 23347712 | tf_op jit(solution)/shard_map/dot_general | solution.py:23
  489.4 18.3 %fusion.69 = bf16[4096,128]{0,1:T(8,128)(2,1)} fusion(bf16[1,4096,2560]{2,1,0:T(8,128)(2,1)} %param.17, bf16[1,4096,2560]{2,1,0:T(8,128)(2,1)} %param.16, f32[2560,128]{0,1:T(8,128)S(1)} %fusion.111, bf16[4096,128]{0,1:T(8,128)(2,1)S(1)} %copy-done.4, f32[4096]{0:T(1024)S(1)} %bitcast.301, f32[128]{0:T(128)S(1)} %add_rsqrt_fusion.3), kind=kOutput, calls=%fused_computation.54 | convolution fusion | flops 5373100032 | bytes 45367808 | tf_op jit(solution)/shard_map/dot_general | solution.py:43
  507.8 24.9 %reduce-scatter.16.cloned.1.call-done = bf16[1024,128]{0,1:T(8,128)(2,1)} async-done(((bf16[4096,128]{0,1:T(8,128)(2,1)}), bf16[1024,128]{0,1:T(8,128)(2,1)}) %reduce-scatter.16.cloned.1.call-update) | async-done | bytes 262160 | tf_op jit(solution)/shard_map/reduce_scatter | solution.py:42
  533.7 3.4 collective-permute-start.4
  537.1 5.4 collective-permute-done.4
  543.5 17.6 %all-gather.19.cloned.1.call-done = bf16[4096,128]{0,1:T(8,128)(2,1)} async-done(((bf16[1024,128]{0,1:T(8,128)(2,1)}), bf16[4096,128]{0,1:T(8,128)(2,1)}) %all-gather.19.cloned.1.call-update) | async-done | bytes 1048592 | tf_op jit(solution)/shard_map/all_gather | solution.py:35
  562.6 8.9 %fusion.117 = f32[2560,128]{0,1:T(8,128)S(1)} fusion(bf16[1,4096,2560]{2,1,0:T(8,128)(2,1)} %param.15, bf16[4096,128]{0,1:T(8,128)(2,1)} %all-gather.19.cloned.1.call-done, f32[4096]{0:T(1024)S(1)} %bitcast.302, f32[128]{0:T(128)S(1)} %add_rsqrt_fusion.2), kind=kOutput, calls=%fused_computation.70 | convolution fusion | flops 2686255104 | bytes 23347712 | tf_op jit(solution)/shard_map/dot_general | solution.py:23
  571.6 18.3 %fusion.66 = bf16[4096,128]{0,1:T(8,128)(2,1)} fusion(bf16[1,4096,2560]{2,1,0:T(8,128)(2,1)} %param.17, bf16[1,4096,2560]{2,1,0:T(8,128)(2,1)} %param.16, f32[2560,128]{0,1:T(8,128)S(1)} %fusion.117, bf16[4096,128]{0,1:T(8,128)(2,1)S(1)} %copy-done.5, f32[4096]{0:T(1024)S(1)} %bitcast.303, f32[128]{0:T(128)S(1)} %add_rsqrt_fusion.2), kind=kOutput, calls=%fused_computation.53 | convolution fusion | flops 5373100032 | bytes 45367808 | tf_op jit(solution)/shard_map/dot_general | solution.py:43
  589.9 24.9 %reduce-scatter.18.cloned.1.call-done = bf16[1024,128]{0,1:T(8,128)(2,1)} async-done(((bf16[4096,128]{0,1:T(8,128)(2,1)}), bf16[1024,128]{0,1:T(8,128)(2,1)}) %reduce-scatter.18.cloned.1.call-update) | async-done | bytes 262160 | tf_op jit(solution)/shard_map/reduce_scatter | solution.py:42
  615.8 3.4 collective-permute-start.5
  619.3 5.4 collective-permute-done.5
  625.4 17.8 %all-gather.21.cloned.1.call-done = bf16[4096,128]{0,1:T(8,128)(2,1)} async-done(((bf16[1024,128]{0,1:T(8,128)(2,1)}), bf16[4096,128]{0,1:T(8,128)(2,1)}) %all-gather.21.cloned.1.call-update) | async-done | bytes 1048592 | tf_op jit(solution)/shard_map/all_gather | solution.py:35
  644.8 8.9 %fusion.123 = f32[2560,128]{0,1:T(8,128)S(1)} fusion(bf16[1,4096,2560]{2,1,0:T(8,128)(2,1)} %param.15, bf16[4096,128]{0,1:T(8,128)(2,1)} %all-gather.21.cloned.1.call-done, f32[4096]{0:T(1024)S(1)} %bitcast.304, f32[128]{0:T(128)S(1)} %add_rsqrt_fusion.1), kind=kOutput, calls=%fused_computation.72 | convolution fusion | flops 2686255104 | bytes 23347712 | tf_op jit(solution)/shard_map/dot_general | solution.py:23
  653.7 18.3 %fusion.63 = bf16[4096,128]{0,1:T(8,128)(2,1)} fusion(bf16[1,4096,2560]{2,1,0:T(8,128)(2,1)} %param.17, bf16[1,4096,2560]{2,1,0:T(8,128)(2,1)} %param.16, f32[2560,128]{0,1:T(8,128)S(1)} %fusion.123, bf16[4096,128]{0,1:T(8,128)(2,1)S(1)} %copy-done.6, f32[4096]{0:T(1024)S(1)} %bitcast.305, f32[128]{0:T(128)S(1)} %add_rsqrt_fusion.1), kind=kOutput, calls=%fused_computation.52 | convolution fusion | flops 5373100032 | bytes 45367808 | tf_op jit(solution)/shard_map/dot_general | solution.py:43
  673.1 23.8 %reduce-scatter.20.cloned.1.call-done = bf16[1024,128]{0,1:T(8,128)(2,1)} async-done(((bf16[4096,128]{0,1:T(8,128)(2,1)}), bf16[1024,128]{0,1:T(8,128)(2,1)}) %reduce-scatter.20.cloned.1.call-update) | async-done | bytes 262160 | tf_op jit(solution)/shard_map/reduce_scatter | solution.py:42
  698.3 10.1 %all-gather = f32[8192,16]{0,1:T(8,128)S(1)} all-gather(f32[1024,16]{0,1:T(8,128)S(1)} %broadcast_multiply_fusion), channel_id=2, replica_groups=mesh['dp'=2,'section'=4,'mp'=4] {'dp','mp'}, dimensions={0}, use_global_device_ids=true | all-gather | bytes 589824 | tf_op jit(solution)/shard_map/all_gather | solution.py:96
  709.6 4.9 fusion.329
  714.7 10.5 %psum.22 = f32[32,32]{1,0:T(8,128)S(1)} all-reduce(f32[32,32]{1,0:T(8,128)S(1)} %fusion.309), channel_id=1, replica_groups=mesh['dp'=2,'section'=4,'mp'=4] {'mp'}, use_global_device_ids=true, to_apply=%region_17.18 | all-reduce | flops 1024 | bytes 8192 | tf_op jit(solution)/shard_map/psum | solution.py:115
  725.2 18.7 %psum.23 = f32[32,32]{1,0:T(8,128)S(1)} all-reduce(f32[32,32]{1,0:T(8,128)S(1)} %broadcast_select_fusion), channel_id=1, replica_groups=mesh['dp'=2,'section'=4,'mp'=4] {'section'}, use_global_device_ids=true, to_apply=%region_18.19 | all-reduce | flops 1024 | bytes 8192 | tf_op jit(solution)/shard_map/psum | solution.py:19
  (131 shorter events, 31.2 us)
Async XLA Ops:
  6.5 118.0 %all-reduce.2.cloned.1.call-start = ((), (), s32[]{:S(2)}) async-start(), calls=%async_computation.7 | async-start | bytes 2097152 | tf_op jit(solution)/shard_map/psum | solution.py:71
  68.5 75.4 %copy-start.7 = (f32[1,4096]{1,0:T(1,128)S(1)}, f32[1,4096]{1,0:T(1,128)}, u32[]{:S(2)}) copy-start(f32[1,4096]{1,0:T(1,128)} %param.14) | copy-start | bytes 49156
  69.8 72.6 %all-gather.9.cloned.1.call-start = ((), (), s32[]{:S(2)}) async-start(), calls=%async_computation.8 | async-start | bytes 1310720 | tf_op jit(solution)/shard_map/all_gather | solution.py:35
  126.3 72.6 %reduce-scatter.8.cloned.1.call-start = ((), (), s32[]{:S(2)}) async-start(), calls=%async_computation.9 | async-start | bytes 1310720 | tf_op jit(solution)/shard_map/reduce_scatter | solution.py:42
  143.9 11.4 %copy-start = (bf16[4096,128]{0,1:T(8,128)(2,1)S(1)}, bf16[4096,128]{0,1:T(8,128)(2,1)}, u32[]{:S(2)}) copy-start(bf16[4096,128]{0,1:T(8,128)(2,1)} %all-gather.9.cloned.1.call-done) | copy-start | bytes 3145732
  155.3 43.5 %copy-start.11 = (bf16[1024,512]{0,1:T(8,128)(2,1)S(1)}, bf16[1024,512]{0,1:T(8,128)(2,1)}, u32[]{:S(2)}) copy-start(bf16[1024,512]{0,1:T(8,128)(2,1)} %all-reduce.2.cloned.1.call-done) | copy-start | bytes 3145732
  173.9 53.4 %all-gather.11.cloned.1.call-start = ((), (), s32[]{:S(2)}) async-start(), calls=%async_computation.10 | async-start | bytes 1310720 | tf_op jit(solution)/shard_map/all_gather | solution.py:35
  199.9 8.8 %collective-permute-start = (bf16[1024,128]{0,1:T(8,128)(2,1)S(1)}, bf16[1024,128]{0,1:T(8,128)(2,1)S(1)}, u32[]{:S(2)}, u32[]{:S(2)}) collective-permute-start(bf16[1024,128]{0,1:T(8,128)(2,1)S(1)} %add_convert_fusion.6), channel_id=1, source_target_pairs={{0,4},{4,8},{8,12},{1,5},{5,9},{9,13},{2,6},{6,10},{10,14},{3,7},{... | collective-permute-start | bytes 786440 | tf_op jit(solution)/shard_map/ppermute | solution.py:14
  209.4 74.2 %reduce-scatter.10.cloned.1.call-start = ((), (), s32[]{:S(2)}) async-start(), calls=%async_computation.11 | async-start | bytes 1310720 | tf_op jit(solution)/shard_map/reduce_scatter | solution.py:42
  228.8 11.4 %copy-start.1 = (bf16[4096,128]{0,1:T(8,128)(2,1)S(1)}, bf16[4096,128]{0,1:T(8,128)(2,1)}, u32[]{:S(2)}) copy-start(bf16[4096,128]{0,1:T(8,128)(2,1)} %all-gather.11.cloned.1.call-done) | copy-start | bytes 3145732
  240.1 43.5 %copy-start.9 = (bf16[1024,128]{0,1:T(8,128)(2,1)S(1)}, bf16[1024,128]{0,1:T(8,128)(2,1)}, u32[]{:S(2)}) copy-start(bf16[1024,128]{0,1:T(8,128)(2,1)} %slice_select_fusion.1) | copy-start | bytes 786436
  258.6 53.4 %all-gather.13.cloned.1.call-start = ((), (), s32[]{:S(2)}) async-start(), calls=%async_computation.12 | async-start | bytes 1310720 | tf_op jit(solution)/shard_map/all_gather | solution.py:35
  284.6 8.8 %collective-permute-start.1 = (bf16[1024,128]{0,1:T(8,128)(2,1)S(1)}, bf16[1024,128]{0,1:T(8,128)(2,1)S(1)}, u32[]{:S(2)}, u32[]{:S(2)}) collective-permute-start(bf16[1024,128]{0,1:T(8,128)(2,1)S(1)} %add_convert_fusion.5), channel_id=1, source_target_pairs={{0,4},{4,8},{8,12},{1,5},{5,9},{9,13},{2,6},{6,10},{10,14},{3,7},{... | collective-permute-start | bytes 786440 | tf_op jit(solution)/shard_map/ppermute | solution.py:14
  294.2 74.2 %reduce-scatter.12.cloned.1.call-start = ((), (), s32[]{:S(2)}) async-start(), calls=%async_computation.13 | async-start | bytes 1310720 | tf_op jit(solution)/shard_map/reduce_scatter | solution.py:42
  313.6 11.4 %copy-start.2 = (bf16[4096,128]{0,1:T(8,128)(2,1)S(1)}, bf16[4096,128]{0,1:T(8,128)(2,1)}, u32[]{:S(2)}) copy-start(bf16[4096,128]{0,1:T(8,128)(2,1)} %all-gather.13.cloned.1.call-done) | copy-start | bytes 3145732
  324.9 43.5 %copy-start.10 = (bf16[1024,128]{0,1:T(8,128)(2,1)S(1)}, bf16[1024,128]{0,1:T(8,128)(2,1)}, u32[]{:S(2)}) copy-start(bf16[1024,128]{0,1:T(8,128)(2,1)} %slice_select_fusion.2) | copy-start | bytes 786436
  343.4 53.4 %all-gather.15.cloned.1.call-start = ((), (), s32[]{:S(2)}) async-start(), calls=%async_computation.14 | async-start | bytes 1310720 | tf_op jit(solution)/shard_map/all_gather | solution.py:35
  369.4 8.8 %collective-permute-start.2 = (bf16[1024,128]{0,1:T(8,128)(2,1)S(1)}, bf16[1024,128]{0,1:T(8,128)(2,1)S(1)}, u32[]{:S(2)}, u32[]{:S(2)}) collective-permute-start(bf16[1024,128]{0,1:T(8,128)(2,1)S(1)} %add_convert_fusion.4), channel_id=1, source_target_pairs={{0,4},{4,8},{8,12},{1,5},{5,9},{9,13},{2,6},{6,10},{10,14},{3,7},{... | collective-permute-start | bytes 786440 | tf_op jit(solution)/shard_map/ppermute | solution.py:14
  378.9 71.6 %reduce-scatter.14.cloned.1.call-start = ((), (), s32[]{:S(2)}) async-start(), calls=%async_computation.15 | async-start | bytes 1310720 | tf_op jit(solution)/shard_map/reduce_scatter | solution.py:42
  398.3 8.9 %copy-start.3 = (bf16[4096,128]{0,1:T(8,128)(2,1)S(1)}, bf16[4096,128]{0,1:T(8,128)(2,1)}, u32[]{:S(2)}) copy-start(bf16[4096,128]{0,1:T(8,128)(2,1)} %all-gather.15.cloned.1.call-done) | copy-start | bytes 3145732
  407.3 43.3 %copy-start.8 = (bf16[1024,128]{0,1:T(8,128)(2,1)S(1)}, bf16[1024,128]{0,1:T(8,128)(2,1)}, u32[]{:S(2)}) copy-start(bf16[1024,128]{0,1:T(8,128)(2,1)} %slice_select_fusion.3) | copy-start | bytes 786436
  425.6 53.3 %all-gather.17.cloned.1.call-start = ((), (), s32[]{:S(2)}) async-start(), calls=%async_computation.16 | async-start | bytes 1310720 | tf_op jit(solution)/shard_map/all_gather | solution.py:35
  451.6 8.8 %collective-permute-start.3 = (bf16[1024,128]{0,1:T(8,128)(2,1)S(1)}, bf16[1024,128]{0,1:T(8,128)(2,1)S(1)}, u32[]{:S(2)}, u32[]{:S(2)}) collective-permute-start(bf16[1024,128]{0,1:T(8,128)(2,1)S(1)} %add_convert_fusion.3), channel_id=1, source_target_pairs={{0,4},{4,8},{8,12},{1,5},{5,9},{9,13},{2,6},{6,10},{10,14},{3,7},{... | collective-permute-start | bytes 786440 | tf_op jit(solution)/shard_map/ppermute | solution.py:14
  460.3 0.7 copy-start.14
  461.1 71.6 %reduce-scatter.16.cloned.1.call-start = ((), (), s32[]{:S(2)}) async-start(), calls=%async_computation.17 | async-start | bytes 1310720 | tf_op jit(solution)/shard_map/reduce_scatter | solution.py:42
  480.5 8.9 %copy-start.4 = (bf16[4096,128]{0,1:T(8,128)(2,1)S(1)}, bf16[4096,128]{0,1:T(8,128)(2,1)}, u32[]{:S(2)}) copy-start(bf16[4096,128]{0,1:T(8,128)(2,1)} %all-gather.17.cloned.1.call-done) | copy-start | bytes 3145732
  489.4 43.3 %copy-start.15 = (bf16[1024,128]{0,1:T(8,128)(2,1)S(1)}, bf16[1024,128]{0,1:T(8,128)(2,1)}, u32[]{:S(2)}) copy-start(bf16[1024,128]{0,1:T(8,128)(2,1)} %copy-done.14) | copy-start | bytes 786436
  507.7 53.4 %all-gather.19.cloned.1.call-start = ((), (), s32[]{:S(2)}) async-start(), calls=%async_computation.18 | async-start | bytes 1310720 | tf_op jit(solution)/shard_map/all_gather | solution.py:35
  533.7 8.8 %collective-permute-start.4 = (bf16[1024,128]{0,1:T(8,128)(2,1)S(1)}, bf16[1024,128]{0,1:T(8,128)(2,1)S(1)}, u32[]{:S(2)}, u32[]{:S(2)}) collective-permute-start(bf16[1024,128]{0,1:T(8,128)(2,1)S(1)} %add_convert_fusion.2), channel_id=1, source_target_pairs={{0,4},{4,8},{8,12},{1,5},{5,9},{9,13},{2,6},{6,10},{10,14},{3,7},{... | collective-permute-start | bytes 786440 | tf_op jit(solution)/shard_map/ppermute | solution.py:14
  542.5 0.7 copy-start.16
  543.2 71.6 %reduce-scatter.18.cloned.1.call-start = ((), (), s32[]{:S(2)}) async-start(), calls=%async_computation.19 | async-start | bytes 1310720 | tf_op jit(solution)/shard_map/reduce_scatter | solution.py:42
  562.6 8.9 %copy-start.5 = (bf16[4096,128]{0,1:T(8,128)(2,1)S(1)}, bf16[4096,128]{0,1:T(8,128)(2,1)}, u32[]{:S(2)}) copy-start(bf16[4096,128]{0,1:T(8,128)(2,1)} %all-gather.19.cloned.1.call-done) | copy-start | bytes 3145732
  571.6 43.2 %copy-start.17 = (bf16[1024,128]{0,1:T(8,128)(2,1)S(1)}, bf16[1024,128]{0,1:T(8,128)(2,1)}, u32[]{:S(2)}) copy-start(bf16[1024,128]{0,1:T(8,128)(2,1)} %copy-done.16) | copy-start | bytes 786436
  589.9 53.3 %all-gather.21.cloned.1.call-start = ((), (), s32[]{:S(2)}) async-start(), calls=%async_computation.20 | async-start | bytes 1310720 | tf_op jit(solution)/shard_map/all_gather | solution.py:35
  615.8 8.8 %collective-permute-start.5 = (bf16[1024,128]{0,1:T(8,128)(2,1)S(1)}, bf16[1024,128]{0,1:T(8,128)(2,1)S(1)}, u32[]{:S(2)}, u32[]{:S(2)}) collective-permute-start(bf16[1024,128]{0,1:T(8,128)(2,1)S(1)} %add_convert_fusion.1), channel_id=1, source_target_pairs={{0,4},{4,8},{8,12},{1,5},{5,9},{9,13},{2,6},{6,10},{10,14},{3,7},{... | collective-permute-start | bytes 786440 | tf_op jit(solution)/shard_map/ppermute | solution.py:14
  624.6 0.7 copy-start.12
  625.4 71.6 %reduce-scatter.20.cloned.1.call-start = ((), (), s32[]{:S(2)}) async-start(), calls=%async_computation.21 | async-start | bytes 1310720 | tf_op jit(solution)/shard_map/reduce_scatter | solution.py:42
  644.7 8.9 %copy-start.6 = (bf16[4096,128]{0,1:T(8,128)(2,1)S(1)}, bf16[4096,128]{0,1:T(8,128)(2,1)}, u32[]{:S(2)}) copy-start(bf16[4096,128]{0,1:T(8,128)(2,1)} %all-gather.21.cloned.1.call-done) | copy-start | bytes 3145732
  653.7 18.4 %copy-start.19 = (s32[32]{0:T(128)S(1)}, s32[32]{0:T(128)}, u32[]{:S(2)}) copy-start(s32[32]{0:T(128)} %param.11) | copy-start | bytes 388
  653.7 18.4 %copy-start.20 = (s32[4]{0:T(128)S(1)}, s32[4]{0:T(128)}, u32[]{:S(2)}) copy-start(s32[4]{0:T(128)} %param.12) | copy-start | bytes 52
  653.7 43.3 %copy-start.13 = (bf16[1024,128]{0,1:T(8,128)(2,1)S(1)}, bf16[1024,128]{0,1:T(8,128)(2,1)}, u32[]{:S(2)}) copy-start(bf16[1024,128]{0,1:T(8,128)(2,1)} %copy-done.12) | copy-start | bytes 786436
  698.3 11.2 %copy-start.18 = (f32[4096]{0:T(1024)S(1)}, f32[4096]{0:T(1024)}, u32[]{:S(2)}) copy-start(f32[4096]{0:T(1024)} %param.18) | copy-start | bytes 49156
Sparse Core Ops, SparseCore 0:
  69.9 54.5 all-reduce.1
  126.4 15.9 all-gather.8
  174.0 24.7 reduce-scatter.7
  209.5 17.6 all-gather.10
  258.8 24.8 reduce-scatter.9
  294.3 17.6 all-gather.12
  343.6 24.7 reduce-scatter.11
  379.1 17.7 all-gather.14
  425.7 24.7 reduce-scatter.13
  461.2 17.6 all-gather.16
  507.9 24.7 reduce-scatter.15
  543.3 17.7 all-gather.18
  590.0 24.7 reduce-scatter.17
  625.5 17.6 all-gather.20
  672.1 24.7 reduce-scatter.19
where the time goes:
time: 761 us; the launch traced here: 752 us
  waiting for transfers between devices  382 us (50%)
  matrix products  204 us (27%)
  local copies, waits for them, and re-layouts  65.8 us (9%)
  blocking collectives  39.3 us (5%)
  other arithmetic  25.4 us (3%)
  starting transfers between devices  21.9 us (3%)
  between operations  14 us (2%)
    reduce_scatter x7, waiting for transfers between devices, layer_split(): lax.psum_scatter(jnp.dot(w_down, hidden, preferred_element_type=jnp.float...  173 us
    dot_general x7, matrix products, layer_split(): jnp.dot(w_down, hidden, preferred_element_type=jnp.float32)  129 us
    all_gather x7, waiting for transfers between devices, layer_split(): wide = lax.all_gather(state, 'mp', axis=0, tiled=True).astype(jnp.float32)  122 us
    dot_general x8, matrix products, contract_rows(): lax.dot_general(weights, acts, (((0,), (0,)), ((), ())), preferred_elemen...  74.6 us
    psum x1, waiting for transfers between devices, per_device(): embedded = lax.psum(partial_value.astype(jnp.bfloat16), 'section')  54.7 us
    unnamed x45, local copies, waits for them, and re-layouts  46.6 us
    ppermute x6, waiting for transfers between devices, passed_along(): lax.ppermute(value, axis, [(source, source + steps) for source in range(l...  32.2 us
    ppermute x6, starting transfers between devices, passed_along(): lax.ppermute(value, axis, [(source, source + steps) for source in range(l...  20.4 us
  transfers between devices with their start and end apart: 21, of which 21 were waited for; matrix products, arithmetic and copies ran while one was open for 0% of the time, Pallas kernels for 0%

commit v1 on v0

--- a/solution.py
+++ b/solution.py
@@ -2,6 +2,7 @@
 import jax.numpy as jnp
 from jax import lax
 from jax.sharding import PartitionSpec as P
+from jax.lax import all_gather
 
 GROUP = 8
 norm_eps = 1e-05
@@ -68,7 +69,8 @@
     inside = (local_ids >= 0) & (local_ids < vocab_part)
     picked = jnp.take(embed_table, jnp.clip(local_ids, 0, vocab_part - 1), axis=1)
     partial_value = jnp.where(inside[None, :], picked.astype(jnp.float32), 0.0)
-    embedded = lax.psum(partial_value.astype(jnp.bfloat16), "section")
+    unit = partial_value.astype(jnp.bfloat16)
+    embedded = jnp.sum(all_gather(unit, "section"), axis=0)
     gain = norm_gain[0]
     w_gate = gate_weight[0]
     w_up = up_weight[0]

time: 761 us -> 785 us (1.032)
  waiting for transfers between devices: 382 us -> 410 us
  matrix products: 204 us -> 196 us
    all_gather x0 -> x1, waiting for transfers between devices: none -> 83.5 us  [per_device(): embedded = jnp.sum(all_gather(unit, 'section'), axis=0)]
    psum x1 -> x0, waiting for transfers between devices: 54.7 us -> none  [per_device(): embedded = lax.psum(partial_value.astype(jnp.bfloat16), 'section')]
    unnamed x45 -> x47, local copies, waits for them, and re-layouts: 46.6 us -> 47.1 us
where the time goes in v1:
time: 785 us; the launch traced here: 776 us
  waiting for transfers between devices  410 us (52%)
  matrix products  196 us (25%)
  local copies, waits for them, and re-layouts  67.9 us (9%)
  blocking collectives  39.3 us (5%)
  other arithmetic  27 us (3%)
  starting transfers between devices  22 us (3%)
  between operations  14.1 us (2%)
    reduce_scatter x7, waiting for transfers between devices, layer_split(): lax.psum_scatter(jnp.dot(w_down, hidden, preferred_element_type=jnp.float...  173 us
    dot_general x7, matrix products, layer_split(): jnp.dot(w_down, hidden, preferred_element_type=jnp.float32)  128 us
    all_gather x7, waiting for transfers between devices, layer_split(): wide = lax.all_gather(state, 'mp', axis=0, tiled=True).astype(jnp.float32)  121 us
    all_gather x1, waiting for transfers between devices, per_device(): embedded = jnp.sum(all_gather(unit, 'section'), axis=0)  83.5 us
    dot_general x8, matrix products, contract_rows(): lax.dot_general(weights, acts, (((0,), (0,)), ((), ())), preferred_elemen...  67.4 us
    unnamed x47, local copies, waits for them, and re-layouts  47.1 us
    ppermute x6, waiting for transfers between devices, passed_along(): lax.ppermute(value, axis, [(source, source + steps) for source in range(l...  31.7 us
    ppermute x6, starting transfers between devices, passed_along(): lax.ppermute(value, axis, [(source, source + steps) for source in range(l...  20.5 us
  transfers between devices with their start and end apart: 21, of which 21 were waited for; matrix products, arithmetic and copies ran while one was open for 0% of the time, Pallas kernels for 0%

profile of v1, /device:TPU:0, one launch (start us, length us, event | category | flops | bytes accessed | tf_op | source)
XLA Modules:
  0.0 775.8 jit_solution(7889346779997077806)
XLA Ops:
  8.2 43.9 %copy.41 = bf16[1024,16384]{0,1:T(8,128)(2,1)} copy(bf16[1024,16384]{1,0:T(8,128)(2,1)} %param.13) | data formatting | bytes 67108864 | tf_op args[3]
  52.1 16.3 %gather_fusion = bf16[512,1024]{1,0:T(8,128)(2,1)S(1)} fusion(bf16[1024,16384]{0,1:T(8,128)(2,1)} %copy.41, s32[1024]{0:T(1024)S(1)} %pad_clamp_fusion.1), kind=kCustom, calls=%fused_computation | custom fusion | bytes 2099200 | tf_op jit(solution)/shard_map/jit(_take)/gather | solution.py:70
  70.2 83.5 %all-gather.10.cloned.1.call-done = bf16[4,1024,512]{2,1,0:T(8,128)(2,1)} async-done(((bf16[1,1024,512]{2,1,0:T(8,128)(2,1)}), bf16[4,1024,512]{2,1,0:T(8,128)(2,1)}) %all-gather.10.cloned.1.call-update) | async-done | bytes 4194320 | tf_op jit(solution)/shard_map/all_gather | solution.py:73
  153.8 3.5 reduce_sum.104
  158.4 15.3 %all-gather.12.cloned.1.call-done = bf16[4096,128]{0,1:T(8,128)(2,1)} async-done(((bf16[1024,128]{0,1:T(8,128)(2,1)}), bf16[4096,128]{0,1:T(8,128)(2,1)}) %all-gather.12.cloned.1.call-update) | async-done | bytes 1048592 | tf_op jit(solution)/shard_map/all_gather | solution.py:36
  175.3 8.9 %fusion.87 = f32[2560,128]{0,1:T(8,128)S(1)} fusion(bf16[1,4096,2560]{2,1,0:T(8,128)(2,1)} %param.15, bf16[4096,128]{0,1:T(8,128)(2,1)} %all-gather.12.cloned.1.call-done, f32[4096]{0:T(1024)S(1)} %bitcast.296, f32[128]{0:T(128)S(1)} %add_rsqrt_fusion.7), kind=kOutput, calls=%fused_computation.60 | convolution fusion | flops 2686255104 | bytes 23347712 | tf_op jit(solution)/shard_map/dot_general | solution.py:24
  184.2 18.3 %fusion.81 = bf16[4096,128]{0,1:T(8,128)(2,1)} fusion(bf16[1,4096,2560]{2,1,0:T(8,128)(2,1)} %param.17, bf16[1,4096,2560]{2,1,0:T(8,128)(2,1)} %param.16, f32[2560,128]{0,1:T(8,128)S(1)} %fusion.87, bf16[4096,128]{0,1:T(8,128)(2,1)S(1)} %copy-done, f32[4096]{0:T(1024)S(1)} %bitcast.297, f32[128]{0:T(128)S(1)} %add_rsqrt_fusion.7), kind=kOutput, calls=%fused_computation.58 | convolution fusion | flops 5373100032 | bytes 45367808 | tf_op jit(solution)/shard_map/dot_general | solution.py:44
  202.6 24.9 %reduce-scatter.8.cloned.1.call-done = bf16[1024,128]{0,1:T(8,128)(2,1)} async-done(((bf16[4096,128]{0,1:T(8,128)(2,1)}), bf16[1024,128]{0,1:T(8,128)(2,1)}) %reduce-scatter.8.cloned.1.call-update) | async-done | bytes 262160 | tf_op jit(solution)/shard_map/reduce_scatter | solution.py:43
  228.5 3.4 collective-permute-start
  232.1 5.2 collective-permute-done
  238.6 17.3 %all-gather.14.cloned.1.call-done = bf16[4096,128]{0,1:T(8,128)(2,1)} async-done(((bf16[1024,128]{0,1:T(8,128)(2,1)}), bf16[4096,128]{0,1:T(8,128)(2,1)}) %all-gather.14.cloned.1.call-update) | async-done | bytes 1048592 | tf_op jit(solution)/shard_map/all_gather | solution.py:36
  257.4 8.9 %fusion.93 = f32[2560,128]{0,1:T(8,128)S(1)} fusion(bf16[1,4096,2560]{2,1,0:T(8,128)(2,1)} %param.15, bf16[4096,128]{0,1:T(8,128)(2,1)} %all-gather.14.cloned.1.call-done, f32[4096]{0:T(1024)S(1)} %bitcast.298, f32[128]{0:T(128)S(1)} %add_rsqrt_fusion.6), kind=kOutput, calls=%fused_computation.62 | convolution fusion | flops 2686255104 | bytes 23347712 | tf_op jit(solution)/shard_map/dot_general | solution.py:24
  266.4 18.3 %fusion.78 = bf16[4096,128]{0,1:T(8,128)(2,1)} fusion(bf16[1,4096,2560]{2,1,0:T(8,128)(2,1)} %param.17, bf16[1,4096,2560]{2,1,0:T(8,128)(2,1)} %param.16, f32[2560,128]{0,1:T(8,128)S(1)} %fusion.93, bf16[4096,128]{0,1:T(8,128)(2,1)S(1)} %copy-done.1, f32[4096]{0:T(1024)S(1)} %bitcast.299, f32[128]{0:T(128)S(1)} %add_rsqrt_fusion.6), kind=kOutput, calls=%fused_computation.57 | convolution fusion | flops 5373100032 | bytes 45367808 | tf_op jit(solution)/shard_map/dot_general | solution.py:44
  284.7 24.9 %reduce-scatter.10.cloned.1.call-done = bf16[1024,128]{0,1:T(8,128)(2,1)} async-done(((bf16[4096,128]{0,1:T(8,128)(2,1)}), bf16[1024,128]{0,1:T(8,128)(2,1)}) %reduce-scatter.10.cloned.1.call-update) | async-done | bytes 262160 | tf_op jit(solution)/shard_map/reduce_scatter | solution.py:43
  310.7 3.4 collective-permute-start.1
  314.3 5.2 collective-permute-done.1
  320.3 17.8 %all-gather.16.cloned.1.call-done = bf16[4096,128]{0,1:T(8,128)(2,1)} async-done(((bf16[1024,128]{0,1:T(8,128)(2,1)}), bf16[4096,128]{0,1:T(8,128)(2,1)}) %all-gather.16.cloned.1.call-update) | async-done | bytes 1048592 | tf_op jit(solution)/shard_map/all_gather | solution.py:36
  339.6 8.9 %fusion.99 = f32[2560,128]{0,1:T(8,128)S(1)} fusion(bf16[1,4096,2560]{2,1,0:T(8,128)(2,1)} %param.15, bf16[4096,128]{0,1:T(8,128)(2,1)} %all-gather.16.cloned.1.call-done, f32[4096]{0:T(1024)S(1)} %bitcast.300, f32[128]{0:T(128)S(1)} %add_rsqrt_fusion.5), kind=kOutput, calls=%fused_computation.64 | convolution fusion | flops 2686255104 | bytes 23347712 | tf_op jit(solution)/shard_map/dot_general | solution.py:24
  348.6 18.3 %fusion.75 = bf16[4096,128]{0,1:T(8,128)(2,1)} fusion(bf16[1,4096,2560]{2,1,0:T(8,128)(2,1)} %param.17, bf16[1,4096,2560]{2,1,0:T(8,128)(2,1)} %param.16, f32[2560,128]{0,1:T(8,128)S(1)} %fusion.99, bf16[4096,128]{0,1:T(8,128)(2,1)S(1)} %copy-done.2, f32[4096]{0:T(1024)S(1)} %bitcast.301, f32[128]{0:T(128)S(1)} %add_rsqrt_fusion.5), kind=kOutput, calls=%fused_computation.56 | convolution fusion | flops 5373100032 | bytes 45367808 | tf_op jit(solution)/shard_map/dot_general | solution.py:44
  366.9 24.9 %reduce-scatter.12.cloned.1.call-done = bf16[1024,128]{0,1:T(8,128)(2,1)} async-done(((bf16[4096,128]{0,1:T(8,128)(2,1)}), bf16[1024,128]{0,1:T(8,128)(2,1)}) %reduce-scatter.12.cloned.1.call-update) | async-done | bytes 262160 | tf_op jit(solution)/shard_map/reduce_scatter | solution.py:43
  392.9 3.4 collective-permute-start.2
  396.4 5.2 collective-permute-done.2
  402.7 17.6 %all-gather.18.cloned.1.call-done = bf16[4096,128]{0,1:T(8,128)(2,1)} async-done(((bf16[1024,128]{0,1:T(8,128)(2,1)}), bf16[4096,128]{0,1:T(8,128)(2,1)}) %all-gather.18.cloned.1.call-update) | async-done | bytes 1048592 | tf_op jit(solution)/shard_map/all_gather | solution.py:36
  421.8 8.9 %fusion.105 = f32[2560,128]{0,1:T(8,128)S(1)} fusion(bf16[1,4096,2560]{2,1,0:T(8,128)(2,1)} %param.15, bf16[4096,128]{0,1:T(8,128)(2,1)} %all-gather.18.cloned.1.call-done, f32[4096]{0:T(1024)S(1)} %bitcast.302, f32[128]{0:T(128)S(1)} %add_rsqrt_fusion.4), kind=kOutput, calls=%fused_computation.66 | convolution fusion | flops 2686255104 | bytes 23347712 | tf_op jit(solution)/shard_map/dot_general | solution.py:24
  430.8 18.3 %fusion.72 = bf16[4096,128]{0,1:T(8,128)(2,1)} fusion(bf16[1,4096,2560]{2,1,0:T(8,128)(2,1)} %param.17, bf16[1,4096,2560]{2,1,0:T(8,128)(2,1)} %param.16, f32[2560,128]{0,1:T(8,128)S(1)} %fusion.105, bf16[4096,128]{0,1:T(8,128)(2,1)S(1)} %copy-done.3, f32[4096]{0:T(1024)S(1)} %bitcast.303, f32[128]{0:T(128)S(1)} %add_rsqrt_fusion.4), kind=kOutput, calls=%fused_computation.55 | convolution fusion | flops 5373100032 | bytes 45367808 | tf_op jit(solution)/shard_map/dot_general | solution.py:44
  449.1 24.9 %reduce-scatter.14.cloned.1.call-done = bf16[1024,128]{0,1:T(8,128)(2,1)} async-done(((bf16[4096,128]{0,1:T(8,128)(2,1)}), bf16[1024,128]{0,1:T(8,128)(2,1)}) %reduce-scatter.14.cloned.1.call-update) | async-done | bytes 262160 | tf_op jit(solution)/shard_map/reduce_scatter | solution.py:43
  475.1 3.4 collective-permute-start.3
  478.5 5.3 collective-permute-done.3
  484.6 17.8 %all-gather.20.cloned.1.call-done = bf16[4096,128]{0,1:T(8,128)(2,1)} async-done(((bf16[1024,128]{0,1:T(8,128)(2,1)}), bf16[4096,128]{0,1:T(8,128)(2,1)}) %all-gather.20.cloned.1.call-update) | async-done | bytes 1048592 | tf_op jit(solution)/shard_map/all_gather | solution.py:36
  504.0 8.9 %fusion.111 = f32[2560,128]{0,1:T(8,128)S(1)} fusion(bf16[1,4096,2560]{2,1,0:T(8,128)(2,1)} %param.15, bf16[4096,128]{0,1:T(8,128)(2,1)} %all-gather.20.cloned.1.call-done, f32[4096]{0:T(1024)S(1)} %bitcast.304, f32[128]{0:T(128)S(1)} %add_rsqrt_fusion.3), kind=kOutput, calls=%fused_computation.68 | convolution fusion | flops 2686255104 | bytes 23347712 | tf_op jit(solution)/shard_map/dot_general | solution.py:24
  512.9 18.3 %fusion.69 = bf16[4096,128]{0,1:T(8,128)(2,1)} fusion(bf16[1,4096,2560]{2,1,0:T(8,128)(2,1)} %param.17, bf16[1,4096,2560]{2,1,0:T(8,128)(2,1)} %param.16, f32[2560,128]{0,1:T(8,128)S(1)} %fusion.111, bf16[4096,128]{0,1:T(8,128)(2,1)S(1)} %copy-done.4, f32[4096]{0:T(1024)S(1)} %bitcast.305, f32[128]{0:T(128)S(1)} %add_rsqrt_fusion.3), kind=kOutput, calls=%fused_computation.54 | convolution fusion | flops 5373100032 | bytes 45367808 | tf_op jit(solution)/shard_map/dot_general | solution.py:44
  531.3 24.9 %reduce-scatter.16.cloned.1.call-done = bf16[1024,128]{0,1:T(8,128)(2,1)} async-done(((bf16[4096,128]{0,1:T(8,128)(2,1)}), bf16[1024,128]{0,1:T(8,128)(2,1)}) %reduce-scatter.16.cloned.1.call-update) | async-done | bytes 262160 | tf_op jit(solution)/shard_map/reduce_scatter | solution.py:43
  557.2 3.4 collective-permute-start.4
  560.6 5.4 collective-permute-done.4
  567.0 17.6 %all-gather.22.cloned.1.call-done = bf16[4096,128]{0,1:T(8,128)(2,1)} async-done(((bf16[1024,128]{0,1:T(8,128)(2,1)}), bf16[4096,128]{0,1:T(8,128)(2,1)}) %all-gather.22.cloned.1.call-update) | async-done | bytes 1048592 | tf_op jit(solution)/shard_map/all_gather | solution.py:36
  586.1 8.9 %fusion.117 = f32[2560,128]{0,1:T(8,128)S(1)} fusion(bf16[1,4096,2560]{2,1,0:T(8,128)(2,1)} %param.15, bf16[4096,128]{0,1:T(8,128)(2,1)} %all-gather.22.cloned.1.call-done, f32[4096]{0:T(1024)S(1)} %bitcast.306, f32[128]{0:T(128)S(1)} %add_rsqrt_fusion.2), kind=kOutput, calls=%fused_computation.70 | convolution fusion | flops 2686255104 | bytes 23347712 | tf_op jit(solution)/shard_map/dot_general | solution.py:24
  595.0 18.3 %fusion.66 = bf16[4096,128]{0,1:T(8,128)(2,1)} fusion(bf16[1,4096,2560]{2,1,0:T(8,128)(2,1)} %param.17, bf16[1,4096,2560]{2,1,0:T(8,128)(2,1)} %param.16, f32[2560,128]{0,1:T(8,128)S(1)} %fusion.117, bf16[4096,128]{0,1:T(8,128)(2,1)S(1)} %copy-done.5, f32[4096]{0:T(1024)S(1)} %bitcast.307, f32[128]{0:T(128)S(1)} %add_rsqrt_fusion.2), kind=kOutput, calls=%fused_computation.53 | convolution fusion | flops 5373100032 | bytes 45367808 | tf_op jit(solution)/shard_map/dot_general | solution.py:44
  613.4 24.9 %reduce-scatter.18.cloned.1.call-done = bf16[1024,128]{0,1:T(8,128)(2,1)} async-done(((bf16[4096,128]{0,1:T(8,128)(2,1)}), bf16[1024,128]{0,1:T(8,128)(2,1)}) %reduce-scatter.18.cloned.1.call-update) | async-done | bytes 262160 | tf_op jit(solution)/shard_map/reduce_scatter | solution.py:43
  639.3 3.4 collective-permute-start.5
  642.7 5.4 collective-permute-done.5
  648.9 17.8 %all-gather.24.cloned.1.call-done = bf16[4096,128]{0,1:T(8,128)(2,1)} async-done(((bf16[1024,128]{0,1:T(8,128)(2,1)}), bf16[4096,128]{0,1:T(8,128)(2,1)}) %all-gather.24.cloned.1.call-update) | async-done | bytes 1048592 | tf_op jit(solution)/shard_map/all_gather | solution.py:36
  668.2 8.9 %fusion.123 = f32[2560,128]{0,1:T(8,128)S(1)} fusion(bf16[1,4096,2560]{2,1,0:T(8,128)(2,1)} %param.15, bf16[4096,128]{0,1:T(8,128)(2,1)} %all-gather.24.cloned.1.call-done, f32[4096]{0:T(1024)S(1)} %bitcast.308, f32[128]{0:T(128)S(1)} %add_rsqrt_fusion.1), kind=kOutput, calls=%fused_computation.72 | convolution fusion | flops 2686255104 | bytes 23347712 | tf_op jit(solution)/shard_map/dot_general | solution.py:24
  677.2 18.3 %fusion.63 = bf16[4096,128]{0,1:T(8,128)(2,1)} fusion(bf16[1,4096,2560]{2,1,0:T(8,128)(2,1)} %param.17, bf16[1,4096,2560]{2,1,0:T(8,128)(2,1)} %param.16, f32[2560,128]{0,1:T(8,128)S(1)} %fusion.123, bf16[4096,128]{0,1:T(8,128)(2,1)S(1)} %copy-done.6, f32[4096]{0:T(1024)S(1)} %bitcast.309, f32[128]{0:T(128)S(1)} %add_rsqrt_fusion.1), kind=kOutput, calls=%fused_computation.52 | convolution fusion | flops 5373100032 | bytes 45367808 | tf_op jit(solution)/shard_map/dot_general | solution.py:44
  696.7 23.8 %reduce-scatter.20.cloned.1.call-done = bf16[1024,128]{0,1:T(8,128)(2,1)} async-done(((bf16[4096,128]{0,1:T(8,128)(2,1)}), bf16[1024,128]{0,1:T(8,128)(2,1)}) %reduce-scatter.20.cloned.1.call-update) | async-done | bytes 262160 | tf_op jit(solution)/shard_map/reduce_scatter | solution.py:43
  721.8 10.1 %all-gather = f32[8192,16]{0,1:T(8,128)S(1)} all-gather(f32[1024,16]{0,1:T(8,128)S(1)} %broadcast_multiply_fusion), channel_id=2, replica_groups=mesh['dp'=2,'section'=4,'mp'=4] {'dp','mp'}, dimensions={0}, use_global_device_ids=true | all-gather | bytes 589824 | tf_op jit(solution)/shard_map/all_gather | solution.py:98
  733.1 4.9 fusion.329
  738.2 10.5 %psum.14 = f32[32,32]{1,0:T(8,128)S(1)} all-reduce(f32[32,32]{1,0:T(8,128)S(1)} %fusion.308), channel_id=1, replica_groups=mesh['dp'=2,'section'=4,'mp'=4] {'mp'}, use_global_device_ids=true, to_apply=%region_17.18 | all-reduce | flops 1024 | bytes 8192 | tf_op jit(solution)/shard_map/psum | solution.py:117
  748.8 18.7 %psum.15 = f32[32,32]{1,0:T(8,128)S(1)} all-reduce(f32[32,32]{1,0:T(8,128)S(1)} %broadcast_select_fusion.4), channel_id=1, replica_groups=mesh['dp'=2,'section'=4,'mp'=4] {'section'}, use_global_device_ids=true, to_apply=%region_18.19 | all-reduce | flops 1024 | bytes 8192 | tf_op jit(solution)/shard_map/psum | solution.py:20
  (136 shorter events, 33.0 us)
Async XLA Ops:
  6.5 147.2 %all-gather.10.cloned.1.call-start = ((), (), s32[]{:S(2)}) async-start(), calls=%async_computation.7 | async-start | bytes 5242880 | tf_op jit(solution)/shard_map/all_gather | solution.py:73
  70.2 103.5 %all-gather.12.cloned.1.call-start = ((), (), s32[]{:S(2)}) async-start(), calls=%async_computation.8 | async-start | bytes 1310720 | tf_op jit(solution)/shard_map/all_gather | solution.py:36
  157.3 18.0 %copy-start.7 = (f32[1,4096]{1,0:T(1,128)S(1)}, f32[1,4096]{1,0:T(1,128)}, u32[]{:S(2)}) copy-start(f32[1,4096]{1,0:T(1,128)} %param.14) | copy-start | bytes 49156
  158.4 69.1 %reduce-scatter.8.cloned.1.call-start = ((), (), s32[]{:S(2)}) async-start(), calls=%async_computation.9 | async-start | bytes 1310720 | tf_op jit(solution)/shard_map/reduce_scatter | solution.py:43
  175.3 8.9 %copy-start = (bf16[4096,128]{0,1:T(8,128)(2,1)S(1)}, bf16[4096,128]{0,1:T(8,128)(2,1)}, u32[]{:S(2)}) copy-start(bf16[4096,128]{0,1:T(8,128)(2,1)} %all-gather.12.cloned.1.call-done) | copy-start | bytes 3145732
  202.5 53.4 %all-gather.14.cloned.1.call-start = ((), (), s32[]{:S(2)}) async-start(), calls=%async_computation.10 | async-start | bytes 1310720 | tf_op jit(solution)/shard_map/all_gather | solution.py:36
  228.5 8.8 %collective-permute-start = (bf16[1024,128]{0,1:T(8,128)(2,1)S(1)}, bf16[1024,128]{0,1:T(8,128)(2,1)S(1)}, u32[]{:S(2)}, u32[]{:S(2)}) collective-permute-start(bf16[1024,128]{0,1:T(8,128)(2,1)S(1)} %add_convert_fusion.6), channel_id=1, source_target_pairs={{0,4},{4,8},{8,12},{1,5},{5,9},{9,13},{2,6},{6,10},{10,14},{3,7},{... | collective-permute-start | bytes 786440 | tf_op jit(solution)/shard_map/ppermute | solution.py:15
  238.1 71.6 %reduce-scatter.10.cloned.1.call-start = ((), (), s32[]{:S(2)}) async-start(), calls=%async_computation.11 | async-start | bytes 1310720 | tf_op jit(solution)/shard_map/reduce_scatter | solution.py:43
  257.4 8.9 %copy-start.1 = (bf16[4096,128]{0,1:T(8,128)(2,1)S(1)}, bf16[4096,128]{0,1:T(8,128)(2,1)}, u32[]{:S(2)}) copy-start(bf16[4096,128]{0,1:T(8,128)(2,1)} %all-gather.14.cloned.1.call-done) | copy-start | bytes 3145732
  266.4 43.3 %copy-start.9 = (bf16[1024,128]{0,1:T(8,128)(2,1)S(1)}, bf16[1024,128]{0,1:T(8,128)(2,1)}, u32[]{:S(2)}) copy-start(bf16[1024,128]{0,1:T(8,128)(2,1)} %broadcast_select_fusion.2) | copy-start | bytes 786436
  284.7 53.4 %all-gather.16.cloned.1.call-start = ((), (), s32[]{:S(2)}) async-start(), calls=%async_computation.12 | async-start | bytes 1310720 | tf_op jit(solution)/shard_map/all_gather | solution.py:36
  310.7 8.8 %collective-permute-start.1 = (bf16[1024,128]{0,1:T(8,128)(2,1)S(1)}, bf16[1024,128]{0,1:T(8,128)(2,1)S(1)}, u32[]{:S(2)}, u32[]{:S(2)}) collective-permute-start(bf16[1024,128]{0,1:T(8,128)(2,1)S(1)} %add_convert_fusion.5), channel_id=1, source_target_pairs={{0,4},{4,8},{8,12},{1,5},{5,9},{9,13},{2,6},{6,10},{10,14},{3,7},{... | collective-permute-start | bytes 786440 | tf_op jit(solution)/shard_map/ppermute | solution.py:15
  320.2 71.6 %reduce-scatter.12.cloned.1.call-start = ((), (), s32[]{:S(2)}) async-start(), calls=%async_computation.13 | async-start | bytes 1310720 | tf_op jit(solution)/shard_map/reduce_scatter | solution.py:43
  339.6 8.9 %copy-start.2 = (bf16[4096,128]{0,1:T(8,128)(2,1)S(1)}, bf16[4096,128]{0,1:T(8,128)(2,1)}, u32[]{:S(2)}) copy-start(bf16[4096,128]{0,1:T(8,128)(2,1)} %all-gather.16.cloned.1.call-done) | copy-start | bytes 3145732
  348.6 43.3 %copy-start.10 = (bf16[1024,128]{0,1:T(8,128)(2,1)S(1)}, bf16[1024,128]{0,1:T(8,128)(2,1)}, u32[]{:S(2)}) copy-start(bf16[1024,128]{0,1:T(8,128)(2,1)} %broadcast_select_fusion.1) | copy-start | bytes 786436
  366.9 53.4 %all-gather.18.cloned.1.call-start = ((), (), s32[]{:S(2)}) async-start(), calls=%async_computation.14 | async-start | bytes 1310720 | tf_op jit(solution)/shard_map/all_gather | solution.py:36
  392.9 8.8 %collective-permute-start.2 = (bf16[1024,128]{0,1:T(8,128)(2,1)S(1)}, bf16[1024,128]{0,1:T(8,128)(2,1)S(1)}, u32[]{:S(2)}, u32[]{:S(2)}) collective-permute-start(bf16[1024,128]{0,1:T(8,128)(2,1)S(1)} %add_convert_fusion.4), channel_id=1, source_target_pairs={{0,4},{4,8},{8,12},{1,5},{5,9},{9,13},{2,6},{6,10},{10,14},{3,7},{... | collective-permute-start | bytes 786440 | tf_op jit(solution)/shard_map/ppermute | solution.py:15
  402.4 71.6 %reduce-scatter.14.cloned.1.call-start = ((), (), s32[]{:S(2)}) async-start(), calls=%async_computation.15 | async-start | bytes 1310720 | tf_op jit(solution)/shard_map/reduce_scatter | solution.py:43
  421.8 8.9 %copy-start.3 = (bf16[4096,128]{0,1:T(8,128)(2,1)S(1)}, bf16[4096,128]{0,1:T(8,128)(2,1)}, u32[]{:S(2)}) copy-start(bf16[4096,128]{0,1:T(8,128)(2,1)} %all-gather.18.cloned.1.call-done) | copy-start | bytes 3145732
  430.8 43.3 %copy-start.8 = (bf16[1024,128]{0,1:T(8,128)(2,1)S(1)}, bf16[1024,128]{0,1:T(8,128)(2,1)}, u32[]{:S(2)}) copy-start(bf16[1024,128]{0,1:T(8,128)(2,1)} %broadcast_select_fusion) | copy-start | bytes 786436
  449.1 53.4 %all-gather.20.cloned.1.call-start = ((), (), s32[]{:S(2)}) async-start(), calls=%async_computation.16 | async-start | bytes 1310720 | tf_op jit(solution)/shard_map/all_gather | solution.py:36
  475.1 8.8 %collective-permute-start.3 = (bf16[1024,128]{0,1:T(8,128)(2,1)S(1)}, bf16[1024,128]{0,1:T(8,128)(2,1)S(1)}, u32[]{:S(2)}, u32[]{:S(2)}) collective-permute-start(bf16[1024,128]{0,1:T(8,128)(2,1)S(1)} %add_convert_fusion.3), channel_id=1, source_target_pairs={{0,4},{4,8},{8,12},{1,5},{5,9},{9,13},{2,6},{6,10},{10,14},{3,7},{... | collective-permute-start | bytes 786440 | tf_op jit(solution)/shard_map/ppermute | solution.py:15
  483.8 0.7 copy-start.13
  484.6 71.6 %reduce-scatter.16.cloned.1.call-start = ((), (), s32[]{:S(2)}) async-start(), calls=%async_computation.17 | async-start | bytes 1310720 | tf_op jit(solution)/shard_map/reduce_scatter | solution.py:43
  504.0 8.9 %copy-start.4 = (bf16[4096,128]{0,1:T(8,128)(2,1)S(1)}, bf16[4096,128]{0,1:T(8,128)(2,1)}, u32[]{:S(2)}) copy-start(bf16[4096,128]{0,1:T(8,128)(2,1)} %all-gather.20.cloned.1.call-done) | copy-start | bytes 3145732
  512.9 43.3 %copy-start.14 = (bf16[1024,128]{0,1:T(8,128)(2,1)S(1)}, bf16[1024,128]{0,1:T(8,128)(2,1)}, u32[]{:S(2)}) copy-start(bf16[1024,128]{0,1:T(8,128)(2,1)} %copy-done.13) | copy-start | bytes 786436
  531.2 53.3 %all-gather.22.cloned.1.call-start = ((), (), s32[]{:S(2)}) async-start(), calls=%async_computation.18 | async-start | bytes 1310720 | tf_op jit(solution)/shard_map/all_gather | solution.py:36
  557.2 8.8 %collective-permute-start.4 = (bf16[1024,128]{0,1:T(8,128)(2,1)S(1)}, bf16[1024,128]{0,1:T(8,128)(2,1)S(1)}, u32[]{:S(2)}, u32[]{:S(2)}) collective-permute-start(bf16[1024,128]{0,1:T(8,128)(2,1)S(1)} %add_convert_fusion.2), channel_id=1, source_target_pairs={{0,4},{4,8},{8,12},{1,5},{5,9},{9,13},{2,6},{6,10},{10,14},{3,7},{... | collective-permute-start | bytes 786440 | tf_op jit(solution)/shard_map/ppermute | solution.py:15
  566.0 0.7 copy-start.15
  566.7 71.6 %reduce-scatter.18.cloned.1.call-start = ((), (), s32[]{:S(2)}) async-start(), calls=%async_computation.19 | async-start | bytes 1310720 | tf_op jit(solution)/shard_map/reduce_scatter | solution.py:43
  586.1 8.9 %copy-start.5 = (bf16[4096,128]{0,1:T(8,128)(2,1)S(1)}, bf16[4096,128]{0,1:T(8,128)(2,1)}, u32[]{:S(2)}) copy-start(bf16[4096,128]{0,1:T(8,128)(2,1)} %all-gather.22.cloned.1.call-done) | copy-start | bytes 3145732
  595.0 43.3 %copy-start.16 = (bf16[1024,128]{0,1:T(8,128)(2,1)S(1)}, bf16[1024,128]{0,1:T(8,128)(2,1)}, u32[]{:S(2)}) copy-start(bf16[1024,128]{0,1:T(8,128)(2,1)} %copy-done.15) | copy-start | bytes 786436
  613.4 53.3 %all-gather.24.cloned.1.call-start = ((), (), s32[]{:S(2)}) async-start(), calls=%async_computation.20 | async-start | bytes 1310720 | tf_op jit(solution)/shard_map/all_gather | solution.py:36
  639.3 8.8 %collective-permute-start.5 = (bf16[1024,128]{0,1:T(8,128)(2,1)S(1)}, bf16[1024,128]{0,1:T(8,128)(2,1)S(1)}, u32[]{:S(2)}, u32[]{:S(2)}) collective-permute-start(bf16[1024,128]{0,1:T(8,128)(2,1)S(1)} %add_convert_fusion.1), channel_id=1, source_target_pairs={{0,4},{4,8},{8,12},{1,5},{5,9},{9,13},{2,6},{6,10},{10,14},{3,7},{... | collective-permute-start | bytes 786440 | tf_op jit(solution)/shard_map/ppermute | solution.py:15
  648.1 0.7 copy-start.11
  648.9 71.6 %reduce-scatter.20.cloned.1.call-start = ((), (), s32[]{:S(2)}) async-start(), calls=%async_computation.21 | async-start | bytes 1310720 | tf_op jit(solution)/shard_map/reduce_scatter | solution.py:43
  668.2 8.9 %copy-start.6 = (bf16[4096,128]{0,1:T(8,128)(2,1)S(1)}, bf16[4096,128]{0,1:T(8,128)(2,1)}, u32[]{:S(2)}) copy-start(bf16[4096,128]{0,1:T(8,128)(2,1)} %all-gather.24.cloned.1.call-done) | copy-start | bytes 3145732
  677.2 18.4 %copy-start.18 = (s32[32]{0:T(128)S(1)}, s32[32]{0:T(128)}, u32[]{:S(2)}) copy-start(s32[32]{0:T(128)} %param.11) | copy-start | bytes 388
  677.2 18.5 %copy-start.19 = (s32[4]{0:T(128)S(1)}, s32[4]{0:T(128)}, u32[]{:S(2)}) copy-start(s32[4]{0:T(128)} %param.12) | copy-start | bytes 52
  677.2 43.3 %copy-start.12 = (bf16[1024,128]{0,1:T(8,128)(2,1)S(1)}, bf16[1024,128]{0,1:T(8,128)(2,1)}, u32[]{:S(2)}) copy-start(bf16[1024,128]{0,1:T(8,128)(2,1)} %copy-done.11) | copy-start | bytes 786436
  721.8 11.2 %copy-start.17 = (f32[4096]{0:T(1024)S(1)}, f32[4096]{0:T(1024)}, u32[]{:S(2)}) copy-start(f32[4096]{0:T(1024)} %param.18) | copy-start | bytes 49156
Sparse Core Ops, SparseCore 0:
  70.3 83.4 all-gather.9
  158.5 15.1 all-gather.11
  202.6 24.8 reduce-scatter.7
  238.2 17.6 all-gather.13
  284.8 24.7 reduce-scatter.9
  320.4 17.6 all-gather.15
  367.0 24.7 reduce-scatter.11
  402.6 17.6 all-gather.17
  449.2 24.8 reduce-scatter.13
  484.7 17.6 all-gather.19
  531.4 24.7 reduce-scatter.15
  566.8 17.7 all-gather.21
  613.5 24.7 reduce-scatter.17
  649.0 17.6 all-gather.23
  695.7 24.7 reduce-scatter.19
